TPU v7x, 256 devices: a whole 4x4x8 slice. The times are simulated.
256 devices in a mesh: seq: 64 (over x, y, z_hi, core), head: 4 (over z_lo).
Axes of the slice: x: 4, y: 4, z: 8 (z_hi: 2, z_lo: 4; z = z_hi * 4 + z_lo), core: 2. Of those that a mesh axis runs over, the one named last changes fastest.
Arguments:
- q_rows: float32 [16384, 2048], P(('seq', 'head')), may hold values from -4 to 4
- k_rows: float32 [16384, 2048], P(('seq', 'head')), may hold values from -4 to 4
- v_rows: float32 [16384, 2048], P(('seq', 'head')), may hold values from -6 to 6
- step_sizes: float32 [8, 16384], P('head', 'seq'), may hold values from 0.1 to 1
- fast_weights: float32 [3, 8, 256, 512], P(None, 'head'), may hold values from -0.375 to 0.375
- norm_gain: float32 [2048], P('head'), may hold values from 0.1 to 1.9
- w_out: bfloat16 [2048, 4096], P('head'), may hold values from -0.125 to 0.125
Outputs:
- mixed_out: bfloat16 [16384, 4096], P(('seq', 'head'))
- new_weights: float32 [3, 8, 256, 512], P(None, 'head')
All inputs are finite; a program needn't handle non-finite values.
Results may differ from a plain program's by a relative error of at most 0.005.
Values sent between devices are 32-bit elements; how exact they have to be, the bound alone decides.
No kernel may reach another device: no remote copies, remote signals or barrier semaphores. Data moves between devices by JAX's collectives and lax.ppermute only.
A program may use at most 128 MiB of HBM per device.

v0:
```python
import math

import jax
import jax.numpy as jnp
from jax import lax
from jax.sharding import PartitionSpec as P

WINDOW = 256
NS_ITERS = 3


highest = lax.Precision.HIGHEST
epsilon = 1e-06
coef_linear = 3.4445
coef_square = -4.775
coef_cubic = 2.0315


def shifted(value, axis, steps):
    count = lax.axis_size(axis)
    first, last = (max(0, -steps), min(count, count - steps))
    return lax.ppermute(value, axis, [(source, source + steps) for source in range(first, last)])


def silu_parts(pre_act):
    sigmoid_gate = jax.nn.sigmoid(pre_act)
    return (pre_act * sigmoid_gate, sigmoid_gate)


def fast_gradients(key_heads, value_heads, step_sizes, weights):
    gate_pre = jnp.einsum("hnd,hdj->hnj", key_heads, weights[0], precision=highest)
    up_pre = jnp.einsum("hnd,hdj->hnj", key_heads, weights[2], precision=highest)
    active, sigmoid_gate = silu_parts(gate_pre)
    glu_out = active * up_pre
    upstream = -step_sizes[:, :, None] * value_heads
    grad_two = jnp.einsum("hnd,hnj->hdj", upstream, glu_out, precision=highest)
    upstream_glu = jnp.einsum("hnd,hdj->hnj", upstream, weights[1], precision=highest)
    grad_three = jnp.einsum("hnd,hnj->hdj", key_heads, upstream_glu * active, precision=highest)
    slope = sigmoid_gate * (1.0 + gate_pre * (1.0 - sigmoid_gate))
    grad_one = jnp.einsum(
        "hnd,hnj->hdj", key_heads, upstream_glu * up_pre * slope, precision=highest
    )
    return jnp.stack([grad_one, grad_two, grad_three])


def orthogonalize(gradients):
    inverse_norm = 1.0 / (
        jnp.sqrt(jnp.sum(gradients * gradients, axis=(2, 3), keepdims=True)) + epsilon
    )
    matrix = gradients * inverse_norm
    for iteration in range(NS_ITERS):
        gram_matrix = jnp.einsum("chdj,chej->chde", matrix, matrix, precision=highest)
        polynomial = coef_square * gram_matrix + coef_cubic * jnp.einsum(
            "chde,chef->chdf", gram_matrix, gram_matrix, precision=highest
        )
        matrix = coef_linear * matrix + jnp.einsum(
            "chde,chej->chdj", polynomial, matrix, precision=highest
        )
    return matrix


def renormalize(old_weights, candidate):
    target = jnp.sqrt(jnp.sum(old_weights * old_weights, axis=2, keepdims=True))
    current = jnp.sqrt(jnp.sum(candidate * candidate, axis=2, keepdims=True)) + epsilon
    return candidate * (target / current)


def local(q_rows, k_rows, v_rows, step_sizes, fast_weights, norm_gain, w_out):
    queries, key_rows, value_rows = (
        lax.all_to_all(q_rows, "head", split_axis=1, concat_axis=0, tiled=True),
        lax.all_to_all(k_rows, "head", split_axis=1, concat_axis=0, tiled=True),
        lax.all_to_all(v_rows, "head", split_axis=1, concat_axis=0, tiled=True),
    )
    length = queries.shape[0]
    heads_here = fast_weights.shape[1]
    head_dim = fast_weights.shape[2]
    key_heads = key_rows.reshape(length, heads_here, head_dim).transpose(1, 0, 2)
    value_heads = value_rows.reshape(length, heads_here, head_dim).transpose(1, 0, 2)
    gradients = fast_gradients(key_heads, value_heads, step_sizes, fast_weights)
    grad_total = lax.psum(gradients, "seq")
    updated = renormalize(fast_weights, fast_weights - orthogonalize(grad_total))
    query_heads = queries.reshape(length, heads_here, head_dim).transpose(1, 0, 2)
    gate_pre = jnp.einsum("hnd,hdj->hnj", query_heads, updated[0], precision=highest)
    up_pre = jnp.einsum("hnd,hdj->hnj", query_heads, updated[2], precision=highest)
    active, sigmoid_gate = silu_parts(gate_pre)
    fast_out = jnp.einsum("hnj,hdj->hnd", active * up_pre, updated[1], precision=highest)
    fast_out = fast_out * lax.rsqrt(jnp.mean(fast_out * fast_out, axis=-1, keepdims=True) + epsilon)
    fast_out = fast_out * norm_gain.reshape(heads_here, 1, head_dim)
    reach_shards = -(-WINDOW // length)
    key_parts = [key_rows]
    value_parts = [value_rows]
    earlier_keys, earlier_values = shifted((key_rows, value_rows), "seq", 1)
    key_parts.insert(0, earlier_keys)
    value_parts.insert(0, earlier_values)
    total_keys = (reach_shards + 1) * length
    all_keys = jnp.concatenate(key_parts, axis=0).reshape(total_keys, heads_here, head_dim)
    all_values = jnp.concatenate(value_parts, axis=0).reshape(total_keys, heads_here, head_dim)
    root = lax.axis_index("seq") * length
    query_pos = root + jnp.arange(length, dtype=jnp.int32)
    key_pos = root - reach_shards * length + jnp.arange(total_keys, dtype=jnp.int32)
    allowed = (
        (key_pos[None, :] <= query_pos[:, None])
        & (key_pos[None, :] > query_pos[:, None] - WINDOW)
        & (key_pos[None, :] >= 0)
    )
    query_rows = queries.reshape(length, heads_here, head_dim)
    scores = jnp.einsum("qhd,khd->hqk", query_rows, all_keys, precision=highest) / math.sqrt(
        head_dim
    )
    scores = jnp.where(allowed[None], scores, -1e30)
    highest_score = jnp.max(scores, axis=-1, keepdims=True)
    expo = jnp.exp(scores - highest_score)
    attention_weights = expo / jnp.sum(expo, axis=-1, keepdims=True)
    attended = jnp.einsum("hqk,khd->qhd", attention_weights, all_values, precision=highest)
    combined = (
        (fast_out.transpose(1, 0, 2) + attended)
        .reshape(length, heads_here * head_dim)
        .astype(jnp.bfloat16)
    )
    mixed_out = lax.psum_scatter(
        jnp.dot(combined, w_out, preferred_element_type=jnp.float32),
        "head",
        scatter_dimension=0,
        tiled=True,
    ).astype(jnp.bfloat16)
    return (mixed_out, updated)


def solution(mesh):
    return jax.shard_map(
        local,
        mesh=mesh,
        in_specs=(
            P(("seq", "head"), None),
            P(("seq", "head"), None),
            P(("seq", "head"), None),
            P("head", "seq"),
            P(None, "head", None, None),
            P("head"),
            P("head", None),
        ),
        out_specs=(P(("seq", "head"), None), P(None, "head", None, None)),
        check_vma=False,
    )
```

profile of v0, /device:TPU:1, one launch (start us, length us, event | category | flops | bytes accessed | tf_op | source)
XLA Modules:
  0.0 1008.7 jit_solution(2499493140897249562)
XLA Ops:
  9.2 6.4 all-to-all-start.1
  17.5 12.3 %all-to-all-done.1 = f32[64,4,512]{2,0,1:T(8,128)} async-done(((f32[64,4,512]{2,0,1:T(8,128)}), f32[64,4,512]{2,0,1:T(8,128)}, u32[]{:S(2)}, u32[]{:S(2)}) %all-to-all-start.1) | async-done | bytes 524320 | tf_op jit(solution)/shard_map/all_to_all | solution.py:71
  29.8 4.1 all-to-all-start
  36.2 3.1 fusion.29
  39.2 3.1 fusion.31
  42.3 5.7 all-to-all-done
  52.4 3.5 convolution_bitcast_fusion.2
  63.8 4.1 all-to-all-start.2
  68.0 2.4 copy.155
  70.4 8.7 collective-permute-start.1
  79.2 2.4 collective-permute-start
  85.7 5.3 collective-permute-done.1
  92.5 8.3 collective-permute-done
  105.0 765.1 %all-reduce.2.cloned.1.call-done = f32[3,2,256,512]{2,3,1,0:T(8,128)} async-done(((f32[3,2,256,512]{2,3,1,0:T(8,128)}), f32[3,2,256,512]{2,3,1,0:T(8,128)}) %all-reduce.2.cloned.1.call-update) | async-done | bytes 3145744 | tf_op jit(solution)/shard_map/psum | solution.py:80
  870.1 2.4 multiply_reduce_fusion.2
  872.9 5.4 fusion.2
  880.0 4.0 multiply_add_fusion.1
  884.0 5.4 fusion.89
  891.0 3.5 multiply_add_fusion
  894.5 5.4 fusion.91
  901.8 4.1 multiply_reduce_fusion
  913.8 3.3 fusion.93
  917.0 2.4 copy.168
  919.4 80.0 %reduce-scatter.2.cloned.1.call-done = f32[64,4096]{1,0:T(8,128)} async-done(((f32[256,4096]{1,0:T(8,128)}), f32[64,4096]{1,0:T(8,128)}) %reduce-scatter.2.cloned.1.call-update) | async-done | bytes 1048592 | tf_op jit(solution)/shard_map/reduce_scatter | solution.py:120
  (75 shorter events, 43.5 us)
Async XLA Ops:
  7.2 26.8 %copy-start.15 = (f32[2,256]{1,0:T(2,128)S(1)}, f32[2,256]{1,0:T(2,128)}, u32[]{:S(2)}) copy-start(f32[2,256]{1,0:T(2,128)} %param.10) | copy-start | bytes 6148
  7.2 29.0 %copy-start = (f32[3,2,256,512]{3,2,1,0:T(8,128)S(1)}, f32[3,2,256,512]{3,2,1,0:T(8,128)}, u32[]{:S(2)}) copy-start(f32[3,2,256,512]{3,2,1,0:T(8,128)} %param.11) | copy-start | bytes 9437188
  9.2 20.6 %all-to-all-start.1 = ((f32[64,4,512]{2,0,1:T(8,128)}), f32[64,4,512]{2,0,1:T(8,128)}, u32[]{:S(2)}, u32[]{:S(2)}) async-start(f32[64,4,512]{2,0,1:T(8,128)} %bitcast.111), calls=%async_computation.1 | async-start | bytes 1048576 | tf_op jit(solution)/shard_map/all_to_all | solution.py:71
  29.8 18.2 %all-to-all-start = ((f32[64,4,512]{2,0,1:T(8,128)}), f32[64,4,512]{2,0,1:T(8,128)}, u32[]{:S(2)}, u32[]{:S(2)}) async-start(f32[64,4,512]{2,0,1:T(8,128)} %bitcast.110), calls=%async_computation | async-start | bytes 1048576 | tf_op jit(solution)/shard_map/all_to_all | solution.py:72
  33.9 836.1 %all-reduce.2.cloned.1.call-start = ((), (), s32[]{:S(2)}) async-start(), calls=%async_computation.4 | async-start | bytes 6291456 | tf_op jit(solution)/shard_map/psum | solution.py:80
  52.3 3.5 copy-start.4
  52.3 3.5 copy-start.11
  52.4 3.5 copy-start.12
  55.9 2.1 copy-start.8
  63.8 20.4 %all-to-all-start.2 = ((f32[64,4,512]{2,0,1:T(8,128)}), f32[64,4,512]{2,0,1:T(8,128)}, u32[]{:S(2)}, u32[]{:S(2)}) async-start(f32[64,4,512]{2,0,1:T(8,128)} %bitcast.109), calls=%async_computation.2 | async-start | bytes 1048576 | tf_op jit(solution)/shard_map/all_to_all | solution.py:70
  68.0 2.4 copy-start.16
  68.0 931.4 %reduce-scatter.2.cloned.1.call-start = ((), (), s32[]{:S(2)}) async-start(), calls=%async_computation.5 | async-start | bytes 5242880 | tf_op jit(solution)/shard_map/reduce_scatter | solution.py:120
  70.4 11.8 %copy-start.5 = (f32[256,2,256]{2,1,0:T(2,128)S(1)}, f32[256,2,256]{2,1,0:T(2,128)}, u32[]{:S(2)}) copy-start(f32[256,2,256]{2,1,0:T(2,128)} %reshape.157) | copy-start | bytes 1572868
  70.4 20.6 %collective-permute-start.1 = (f32[256,512]{1,0:T(8,128)}, f32[256,512]{1,0:T(8,128)}, u32[]{:S(2)}, u32[]{:S(2)}) collective-permute-start(f32[256,512]{1,0:T(8,128)} %bitcast.23), channel_id=1, source_target_pairs={{0,4},{4,8},{8,12},{12,16},{16,20},{20,24},{24,28},{28,32},{32,36}... | collective-permute-start | bytes 1572872 | tf_op jit(solution)/shard_map/ppermute | solution.py:22
  79.2 21.6 %collective-permute-start = (f32[256,512]{1,0:T(8,128)}, f32[256,512]{1,0:T(8,128)}, u32[]{:S(2)}, u32[]{:S(2)}) collective-permute-start(f32[256,512]{1,0:T(8,128)} %bitcast.21), channel_id=1, source_target_pairs={{0,4},{4,8},{8,12},{12,16},{16,20},{20,24},{24,28},{28,32},{32,36}... | collective-permute-start | bytes 1572872 | tf_op jit(solution)/shard_map/ppermute | solution.py:22
  85.7 18.5 %copy-start.6 = (f32[256,2,256]{2,1,0:T(2,128)}, f32[256,2,256]{2,1,0:T(2,128)S(1)}, u32[]{:S(2)}) copy-start(f32[256,2,256]{2,1,0:T(2,128)S(1)} %reshape.158) | copy-start | bytes 1572868
  104.0 1.0 copy-start.9
  870.1 2.8 copy-start.1
  899.9 1.9 copy-start.2
  906.0 1.0 copy-start.7
  908.1 3.5 copy-start.10
  908.1 3.5 copy-start.13
  908.1 3.5 copy-start.14
  911.6 2.2 copy-start.3
Sparse Core Ops, SparseCore 0:
  62.1 807.9 all-reduce.1
  917.2 82.1 reduce-scatter.1
where the time goes:
time: 1020 us; the launch traced here: 1010 us
  waiting for transfers between devices  877 us (86%)
  matrix products  58.8 us (6%)
  starting transfers between devices  25.9 us (3%)
  local copies, waits for them, and re-layouts  24.7 us (2%)
  between operations  14.9 us (1%)
    psum x1, waiting for transfers between devices, local(): grad_total = lax.psum(gradients, 'seq')  765 us
    reduce_scatter x1, waiting for transfers between devices, local(): lax.psum_scatter(jnp.dot(combined, w_out, preferred_element_type=jnp.floa...  80 us
  transfers between devices with their start and end apart: 7, of which 6 were waited for; matrix products, arithmetic and copies ran while one was open for 3% of the time, Pallas kernels for 0%

commit v1 on v0

v1 whole, which is shorter than its diff:
```python
import math
import jax
import jax.numpy as jnp
from jax import lax
from jax.experimental import pallas as pl
from jax.experimental.pallas import tpu as pltpu
from jax.sharding import Mesh, PartitionSpec as P


NS_ITERS = 3
epsilon = 1e-06
coef_linear = 3.4445
coef_square = -4.775
coef_cubic = 2.0315


def split(value):
    high = value.astype(jnp.bfloat16)
    low = (value - high.astype(jnp.float32)).astype(jnp.bfloat16)
    return high, low


def dot3(left, right, contract):
    dims = (contract, ((), ()))
    (lh, ll), (rh, rl) = left, right
    prod = lambda a, b: lax.dot_general(a, b, dims, preferred_element_type=jnp.float32)
    return prod(lh, rh) + (prod(lh, rl) + prod(ll, rh))


NN = ((1,), (0,))
NT = ((1,), (1,))
TN = ((0,), (0,))


def rows_of(ref):
    return ref[...].reshape(-1, ref.shape[-1])


def joined(*refs):
    return jnp.concatenate([ref[...] for ref in refs], axis=0)


def gradient_kernel(k_ref, v_ref, s_ref, w_ref, g_ref):
    key = split(rows_of(k_ref))
    upstream = split(-s_ref[...] * rows_of(v_ref))
    gate_pre = dot3(key, split(w_ref[0]), NN)
    up_pre = dot3(key, split(w_ref[2]), NN)
    back = dot3(upstream, split(w_ref[1]), NN)
    sig = jax.nn.sigmoid(gate_pre)
    active = gate_pre * sig
    g_ref[1] = dot3(upstream, split(active * up_pre), TN)
    g_ref[2] = dot3(key, split(back * active), TN)
    slope = sig * (1.0 + gate_pre * (1.0 - sig))
    g_ref[0] = dot3(key, split(back * up_pre * slope), TN)


def newton_kernel(g_ref, w_ref, o_ref):
    mats = []
    for i in range(3):
        g = g_ref[i]
        mats.append(g * (1.0 / (jnp.sqrt(jnp.sum(g * g, keepdims=True)) + epsilon)))
    for _ in range(NS_ITERS):
        parts = [split(m) for m in mats]
        grams = [dot3(p, p, NT) for p in parts]
        gparts = [split(a) for a in grams]
        polys = [coef_square * a + coef_cubic * dot3(p, p, NN) for a, p in zip(grams, gparts)]
        mats = [coef_linear * m + dot3(split(b), p, NN) for m, b, p in zip(mats, polys, parts)]
    for i in range(3):
        w = w_ref[i]
        c = w - mats[i]
        target = jnp.sqrt(jnp.sum(w * w, axis=0, keepdims=True))
        current = jnp.sqrt(jnp.sum(c * c, axis=0, keepdims=True)) + epsilon
        o_ref[i] = c * (target / current)


def attention_kernel(first_ref, order_ref, qa, qb, qc, qd, kp_ref, k_ref, vp_ref, v_ref, o_ref):
    q = split(joined(qa, qb, qc, qd))
    scale = 1.0 / math.sqrt(o_ref.shape[-1])
    prev = dot3(q, split(rows_of(kp_ref)), NT) * scale
    here = dot3(q, split(rows_of(k_ref)), NT) * scale
    row = lax.broadcasted_iota(jnp.int32, prev.shape, 0)
    col = lax.broadcasted_iota(jnp.int32, prev.shape, 1)
    prev = jnp.where((col > row) & (first_ref[0] > 0), prev, -1e30)
    here = jnp.where(col <= row, here, -1e30)
    top = jnp.maximum(jnp.max(prev, axis=1, keepdims=True), jnp.max(here, axis=1, keepdims=True))
    ep, eh = jnp.exp(prev - top), jnp.exp(here - top)
    total = jnp.sum(ep, axis=1, keepdims=True) + jnp.sum(eh, axis=1, keepdims=True)
    acc = dot3(split(ep), split(rows_of(vp_ref)), NN) + dot3(split(eh), split(rows_of(v_ref)), NN)
    o_ref[...] = acc / total


def apply_head(qa, qb, qc, qd, w_ref, att_ref, gain_ref):
    q = split(joined(qa, qb, qc, qd))
    gate_pre = dot3(q, split(w_ref[0]), NN)
    up_pre = dot3(q, split(w_ref[2]), NN)
    glu = gate_pre * jax.nn.sigmoid(gate_pre) * up_pre
    fast = dot3(split(glu), split(w_ref[1]), NT)
    fast = fast * lax.rsqrt(jnp.mean(fast * fast, axis=1, keepdims=True) + epsilon)
    return fast * gain_ref[...] + att_ref[...]


def apply_first_kernel(head_ref, order_ref, *refs):
    *given, o_ref = refs
    o_ref[...] = apply_head(*given)


def apply_second_kernel(head_ref, order_ref, *refs):
    *given, done_ref, o_ref = refs
    value = apply_head(*given)
    done = done_ref[...]
    is_first = head_ref[0] == 0
    dim = value.shape[1]
    o_ref[:, :dim] = jnp.where(is_first, value, done).astype(o_ref.dtype)
    o_ref[:, dim:] = jnp.where(is_first, done, value).astype(o_ref.dtype)


SEQ = ("x", "y", "zh", "core")
HEAD_DIM = 256


def head_gradient(pairs, steps, weights, head):
    dim, hidden = weights.shape[2:]
    length = steps.shape[1]
    ranks, _, rows, _ = pairs.shape
    spec = pltpu.PrefetchScalarGridSpec(
        num_scalar_prefetch=1,
        grid=(1,),
        in_specs=[
            pl.BlockSpec((ranks, None, rows, dim), lambda i, h: (0, 0, 0, h[0])),
            pl.BlockSpec((ranks, None, rows, dim), lambda i, h: (0, 1, 0, h[0])),
            pl.BlockSpec((None, length, 1), lambda i, h: (h[0], 0, 0)),
            pl.BlockSpec((3, None, dim, hidden), lambda i, h: (0, h[0], 0, 0)),
        ],
        out_specs=pl.BlockSpec((3, dim, hidden), lambda i, h: (0, 0, 0)),
    )
    return pl.pallas_call(
        lambda h, *refs: gradient_kernel(*refs),
        grid_spec=spec,
        out_shape=jax.ShapeDtypeStruct((3, dim, hidden), jnp.float32),
        name="gradient",
    )(head, pairs, pairs, steps, weights)


def newton(grads, weights, head):
    _, dim, hidden = grads.shape
    spec = pltpu.PrefetchScalarGridSpec(
        num_scalar_prefetch=1,
        grid=(1,),
        in_specs=[
            pl.BlockSpec((3, dim, hidden), lambda i, h: (0, 0, 0)),
            pl.BlockSpec((3, None, dim, hidden), lambda i, h: (0, h[0], 0, 0)),
        ],
        out_specs=pl.BlockSpec((3, dim, hidden), lambda i, h: (0, 0, 0)),
    )
    return pl.pallas_call(
        lambda h, *refs: newton_kernel(*refs),
        grid_spec=spec,
        out_shape=jax.ShapeDtypeStruct((3, dim, hidden), jnp.float32),
        name="newton",
    )(head, grads, weights)


def query_specs(rows, dim, column):
    def block(source):
        return pl.BlockSpec(
            (None, rows, dim), lambda i, f, order: (order[source], 0, column(i, f))
        )

    return [block(source) for source in range(4)]


def attention(first, order, queries, before, pairs):
    ranks, _, rows, width = pairs.shape
    dim = HEAD_DIM
    length = ranks * rows
    key = pl.BlockSpec((ranks, None, rows, dim), lambda i, f, order: (0, 0, 0, i))
    value = pl.BlockSpec((ranks, None, rows, dim), lambda i, f, order: (0, 1, 0, i))
    return pl.pallas_call(
        attention_kernel,
        grid_spec=pltpu.PrefetchScalarGridSpec(
            num_scalar_prefetch=2,
            grid=(width // dim,),
            in_specs=[*query_specs(rows, dim, lambda i, f: i), key, key, value, value],
            out_specs=pl.BlockSpec((length, dim), lambda i, f, order: (0, i)),
        ),
        out_shape=jax.ShapeDtypeStruct((length, width), jnp.float32),
        name="attention",
    )(first, order, *[queries] * 4, before, pairs, before, pairs)


def apply_fast(head, order, queries, weights, attended, gain, done=None):
    ranks, rows, width = queries.shape
    length = ranks * rows
    _, dim, hidden = weights.shape
    specs = [
        *query_specs(rows, dim, lambda i, h: h[0]),
        pl.BlockSpec((3, dim, hidden), lambda i, h, order: (0, 0, 0)),
        pl.BlockSpec((length, dim), lambda i, h, order: (0, h[0])),
        pl.BlockSpec((1, dim), lambda i, h, order: (0, h[0])),
    ]
    if done is not None:
        specs.append(pl.BlockSpec((length, dim), lambda i, h, order: (0, 0)))
    extent = dim if done is None else width
    return pl.pallas_call(
        apply_first_kernel if done is None else apply_second_kernel,
        grid_spec=pltpu.PrefetchScalarGridSpec(
            num_scalar_prefetch=2,
            grid=(1,),
            in_specs=specs,
            out_specs=pl.BlockSpec((length, extent), lambda i, h, order: (0, 0)),
        ),
        out_shape=jax.ShapeDtypeStruct(
            (length, extent), jnp.float32 if done is None else jnp.bfloat16
        ),
        name="apply_first" if done is None else "apply_second",
    )(head, order, *[queries] * 4, weights, attended, gain, *(() if done is None else (done,)))


def by_head(rows):
    length, width = rows.shape
    return rows.reshape(length, 4, width // 4).transpose(1, 0, 2)


def exchange(value, axes):
    return lax.all_to_all(value, axes, split_axis=0, concat_axis=0, tiled=True)


def rotated_heads(rows):
    width = rows.shape[1] // 4
    here = lax.axis_index("head")
    parts = []
    for step in range(4):
        column = lax.rem(here + step, 4) * width
        part = lax.dynamic_slice_in_dim(rows, column, width, axis=1)
        if step:
            part = lax.ppermute(part, "head", [(rank, (rank + step) % 4) for rank in range(4)])
        parts.append(part)
    order = jnp.stack([lax.rem(here + 4 - source, 4) for source in range(4)])
    return jnp.stack(parts), order


def swap_cores(value):
    return lax.ppermute(value, "core", [(0, 1), (1, 0)])


def sum_rest(value):
    shape = value.shape
    pieces = exchange(value.reshape(16, -1, shape[-1]), ("x", "y"))
    part = jnp.sum(pieces, axis=0)
    part = part + lax.ppermute(part, "zh", [(0, 1), (1, 0)])
    return exchange(jnp.broadcast_to(part, (16, *part.shape)), ("x", "y")).reshape(shape)


def earlier(value):
    return lax.ppermute(value, SEQ, [(source, source + 1) for source in range(63)])


def local(q_rows, k_rows, v_rows, step_sizes, fast_weights, norm_gain, w_out):
    core = lax.axis_index("core")
    mine, other = core.reshape(1), (1 - core).reshape(1)
    first = lax.axis_index(SEQ).reshape(1)
    steps = step_sizes[:, :, None]
    gain = norm_gain.reshape(1, -1)
    pairs = exchange(jnp.stack([by_head(k_rows), by_head(v_rows)], axis=1), "head")
    given = head_gradient(pairs, steps, fast_weights, other)
    received = swap_cores(given)
    kept = head_gradient(pairs, steps, fast_weights, mine)
    before = earlier(pairs)
    total = sum_rest(kept + received)
    updated = newton(total, fast_weights, mine)
    partner = swap_cores(updated)
    queries, order = rotated_heads(q_rows)
    attended = attention(first, order, queries, before, pairs)
    done = apply_fast(mine, order, queries, updated, attended, gain)
    combined = apply_fast(other, order, queries, partner, attended, gain, done)
    partial = jnp.dot(combined, w_out, preferred_element_type=jnp.float32)
    mixed = lax.psum_scatter(partial, "head", scatter_dimension=0, tiled=True)
    own, swapped = updated[:, None], partner[:, None]
    new_weights = jnp.where(
        core == 0,
        jnp.concatenate([own, swapped], axis=1),
        jnp.concatenate([swapped, own], axis=1),
    )
    return (mixed.astype(jnp.bfloat16), new_weights)


def solution(mesh):
    mesh = Mesh(mesh.devices.reshape(4, 4, 2, 2, 4), (*SEQ, "head"))
    return jax.shard_map(
        local,
        mesh=mesh,
        in_specs=(
            P((*SEQ, "head"), None),
            P((*SEQ, "head"), None),
            P((*SEQ, "head"), None),
            P("head", SEQ),
            P(None, "head", None, None),
            P("head"),
            P("head", None),
        ),
        out_specs=(P((*SEQ, "head"), None), P(None, "head", None, None)),
        check_vma=False,
    )
```

time: 1020 us -> 276 us (0.27); the launches traced: 1010 us -> 275 us
  waiting for transfers between devices: 877 us -> 128 us
  matrix products: 58.8 us -> 5.49 us
  blocking collectives: 0 us -> 49.8 us
  Pallas kernels: 0 us -> 31.3 us
  local copies, waits for them, and re-layouts: 24.7 us -> 8.84 us
    psum x1 -> x0, waiting for transfers between devices: 765 us -> none  [local(): grad_total = lax.psum(gradients, 'seq')]
    dot_general x21 -> x1, matrix products: 58.8 us -> 5.49 us  [local(): partial = jnp.dot(combined, w_out, preferred_element_type=jnp.float32)]
    all_to_all x0 -> x2, blocking collectives: none -> 49.8 us  [exchange(): return lax.all_to_all(value, axes, split_axis=0, concat_axis=0, tiled=True)]
    pallas_call x0 -> x6, Pallas kernels: none -> 31.3 us  [the longest x1 8.9 us: newton(): pl.pallas_call(lambda h, *refs: newton_kernel(*refs), grid_spec=spec, out...]
    ppermute x2 -> x7, waiting for transfers between devices: 13.7 us -> 31.6 us  [the longest x3 28.9 us: rotated_heads(): lax.ppermute(part, 'head', [(rank, (rank + step) % 4) for rank in range(4)])]
    ppermute x2 -> x7, starting transfers between devices: 11.1 us -> 22.1 us  [the longest x2 7.35 us: swap_cores(): return lax.ppermute(value, 'core', [(0, 1), (1, 0)])]
    all_to_all x3 -> x1, waiting for transfers between devices: 18 us -> 24.4 us  [exchange(): return lax.all_to_all(value, axes, split_axis=0, concat_axis=0, tiled=True)]
  transfers between devices with their start and end apart: 7 -> 9, of which waited for: 6 -> 5; matrix products, arithmetic and copies ran while one was open for 3% -> 3% of each run, Pallas kernels for 0% -> 5%
where the time goes in v1:
time: 276 us; the launch traced here: 275 us
  waiting for transfers between devices  128 us (46%)
  blocking collectives  49.8 us (18%)
  Pallas kernels  31.3 us (11%)
  starting transfers between devices  28.6 us (10%)
  between operations  14.1 us (5%)
  other arithmetic  8.86 us (3%)
  local copies, waits for them, and re-layouts  8.84 us (3%)
  matrix products  5.49 us (2%)
    reduce_scatter x1, waiting for transfers between devices, local(): mixed = lax.psum_scatter(partial, 'head', scatter_dimension=0, tiled=True)  71.9 us
    all_to_all x2, blocking collectives, exchange(): return lax.all_to_all(value, axes, split_axis=0, concat_axis=0, tiled=True)  49.8 us
    ppermute x3, waiting for transfers between devices, rotated_heads(): lax.ppermute(part, 'head', [(rank, (rank + step) % 4) for rank in range(4)])  28.9 us
    all_to_all x1, waiting for transfers between devices, exchange(): return lax.all_to_all(value, axes, split_axis=0, concat_axis=0, tiled=True)  24.4 us
    pallas_call x1, Pallas kernels, newton(): pl.pallas_call(lambda h, *refs: newton_kernel(*refs), grid_spec=spec, out...  8.9 us
    pallas_call x2, Pallas kernels, head_gradient(): pl.pallas_call(lambda h, *refs: gradient_kernel(*refs), grid_spec=spec, o...  8.66 us
    pallas_call x2, Pallas kernels, apply_fast(): pl.pallas_call(apply_first_kernel if done is None else apply_second_kerne...  8.56 us
    ppermute x2, starting transfers between devices, swap_cores(): return lax.ppermute(value, 'core', [(0, 1), (1, 0)])  7.35 us
  transfers between devices with their start and end apart: 9, of which 5 were waited for; matrix products, arithmetic and copies ran while one was open for 3% of the time, Pallas kernels for 5%

profile of v1, /device:TPU:1, one launch (start us, length us, event | category | flops | bytes accessed | tf_op | source)
XLA Modules:
  0.0 274.9 jit_solution(4861724570633503108)
XLA Ops:
  9.5 6.4 %all-to-all-start = ((f32[4,2,64,512]{3,2,1,0:T(8,128)}), f32[4,2,64,512]{3,2,1,0:T(8,128)S(1)}, u32[]{:S(2)}, u32[]{:S(2)}) async-start(f32[4,2,64,512]{3,2,1,0:T(8,128)} %pad_maximum_fusion), calls=%async_computation | async-start | bytes 2097152 | tf_op jit(solution)/shard_map/all_to_all | solution.py:225
  16.8 24.4 %all-to-all-done.refs_0_.refs_1_.k_ref.v_ref = f32[4,2,64,512]{3,2,1,0:T(8,128)S(1)} async-done(((f32[4,2,64,512]{3,2,1,0:T(8,128)}), f32[4,2,64,512]{3,2,1,0:T(8,128)S(1)}, u32[]{:S(2)}, u32[]{:S(2)}) %all-to-all-start) | async-done | bytes 1048608 | tf_op jit(solution)/shard_map/all_to_all | solution.py:225
  42.2 4.3 %gradient.3 = f32[3,256,512]{2,1,0:T(8,128)} custom-call(s32[1]{0:T(128)} %bitcast.h.head_ref, f32[4,2,64,512]{3,2,1,0:T(8,128)} %copy-done, f32[4,2,64,512]{3,2,1,0:T(8,128)} %copy-done, f32[2,256,1]{2,1,0:T(8,128)} %copy.12.refs_2_, f32[3,2,256,512]{3,2,1,0:T(8,128)} %refs_1_.1), custom_call_target="tpu_custom_call" | custom-call | tf_op jit(solution)/shard_map/gradient/pallas_call | solution.py:136
  46.5 1.4 collective-permute-start.3
  47.9 4.3 %gradient.2 = f32[3,256,512]{2,1,0:T(8,128)} custom-call(s32[1]{0:T(128)} %bitcast.9.h.head_ref, f32[4,2,64,512]{3,2,1,0:T(8,128)} %copy-done, f32[4,2,64,512]{3,2,1,0:T(8,128)} %copy-done, f32[2,256,1]{2,1,0:T(8,128)} %copy.12.refs_2_, f32[3,2,256,512]{3,2,1,0:T(8,128)} %refs_1_.1), custom_call_target="tpu_custom_call" | custom-call | tf_op jit(solution)/shard_map/gradient/pallas_call | solution.py:136
  52.3 1.8 add.52
  54.0 27.9 %all_to_all.15 = f32[16,48,512]{2,1,0:T(8,128)S(1)} all-to-all(f32[16,48,512]{2,1,0:T(8,128)S(1)} %bitcast.35), channel_id=1, replica_groups=mesh['x'=4,'y'=4,'zh'=2,'core'=2,'head'=4] {'x','y'}, dimensions={0} | all-to-all | bytes 3145728 | tf_op jit(solution)/shard_map/all_to_all | solution.py:225
  82.1 4.9 %collective-permute-start.4 = (f32[48,512]{1,0:T(8,128)S(1)}, f32[48,512]{1,0:T(8,128)S(1)}, u32[]{:S(2)}, u32[]{:S(2)}) collective-permute-start(f32[48,512]{1,0:T(8,128)S(1)} %reduce_sum.9), channel_id=1, source_target_pairs={{0,8},{8,0},{1,9},{9,1},{2,10},{10,2},{3,11},{11,3},{4,12},{12,4},... | collective-permute-start | bytes 294920 | tf_op jit(solution)/shard_map/ppermute | solution.py:250
  86.9 2.7 collective-permute-done.4
  89.8 21.9 %all_to_all.16 = f32[16,48,512]{2,1,0:T(8,128)} all-to-all(f32[16,48,512]{2,1,0:T(8,128)S(1)} %broadcast_in_dim.13), channel_id=1, replica_groups=mesh['x'=4,'y'=4,'zh'=2,'core'=2,'head'=4] {'x','y'}, dimensions={0} | all-to-all | bytes 3145728 | tf_op jit(solution)/shard_map/all_to_all | solution.py:225
  111.7 8.9 %newton.1.refs_4_ = f32[3,256,512]{2,1,0:T(8,128)} custom-call(s32[1]{0:T(128)} %bitcast.9.h.head_ref, f32[3,256,512]{2,1,0:T(8,128)} %bitcast.36, f32[3,2,256,512]{3,2,1,0:T(8,128)} %refs_1_.1), custom_call_target="tpu_custom_call" | custom-call | tf_op jit(solution)/shard_map/newton/pallas_call | solution.py:155
  120.6 6.0 %collective-permute-start.5 = (f32[3,256,512]{2,1,0:T(8,128)}, f32[3,256,512]{2,1,0:T(8,128)S(1)}, u32[]{:S(2)}, u32[]{:S(2)}) collective-permute-start(f32[3,256,512]{2,1,0:T(8,128)} %newton.1.refs_4_), channel_id=1, source_target_pairs={{0,4},{4,0},{1,5},{5,1},{2,6},{6,2},{3,7},{7,3},{8,12},{12,8},{9,1... | collective-permute-start | bytes 4718600 | tf_op jit(solution)/shard_map/ppermute | solution.py:243
  126.6 6.6 %collective-permute-start.6 = (f32[4,2,64,512]{3,2,1,0:T(8,128)S(1)}, f32[4,2,64,512]{3,2,1,0:T(8,128)}, u32[]{:S(2)}, u32[]{:S(2)}) collective-permute-start(f32[4,2,64,512]{3,2,1,0:T(8,128)S(1)} %copy-done.1), channel_id=1, source_target_pairs={{0,4},{4,8},{8,12},{12,16},{16,20},{20,24},{24,28},{28,32},{32,36}... | collective-permute-start | bytes 3145736 | tf_op jit(solution)/shard_map/ppermute | solution.py:255
  134.0 3.3 %collective-permute-start.2 = (f32[64,512]{1,0:T(8,128)S(1)}, f32[64,512]{1,0:T(8,128)S(1)}, u32[]{:S(2)}, u32[]{:S(2)}) collective-permute-start(f32[64,512]{1,0:T(8,128)S(1)} %get-tuple-element.8), channel_id=1, source_target_pairs={{0,3},{1,0},{2,1},{3,2},{4,7},{5,4},{6,5},{7,6},{8,11},{9,8},{10,9... | collective-permute-start | bytes 393224 | tf_op jit(solution)/shard_map/ppermute | solution.py:236
  137.8 23.2 %collective-permute-done = f32[64,512]{1,0:T(8,128)S(1)} collective-permute-done((f32[64,512]{1,0:T(8,128)}, f32[64,512]{1,0:T(8,128)S(1)}, u32[]{:S(2)}, u32[]{:S(2)}) %collective-permute-start) | collective-permute-done | bytes 131104 | tf_op jit(solution)/shard_map/ppermute | solution.py:236
  161.0 5.8 %collective-permute-done.1 = f32[64,512]{1,0:T(8,128)S(1)} collective-permute-done((f32[64,512]{1,0:T(8,128)S(1)}, f32[64,512]{1,0:T(8,128)S(1)}, u32[]{:S(2)}, u32[]{:S(2)}) %collective-permute-start.1) | collective-permute-done | bytes 131104 | tf_op jit(solution)/shard_map/ppermute | solution.py:236
  167.6 5.2 %attention.1.refs_5_ = f32[256,512]{1,0:T(8,128)} custom-call(s32[1]{0:T(128)} %bitcast.17.first_ref, s32[4]{0:T(128)} %pad_add_fusion.order_ref, f32[4,64,512]{2,1,0:T(8,128)} %pad_maximum_fusion.1.qa.qb.qc.qd.refs_0_.refs_1_.refs_2_.refs_3_, f32[4,64,512]{2,1,0:T(8,128)} %pad_maximum_fusion.1.qa.qb.qc.qd.refs_0_.refs_1_.refs_2_.refs_3_, ...), custom_call_target="tpu_custom_call" | custom-call | tf_op jit(solution)/shard_map/attention/pallas_call | solution.py:178
  172.8 4.3 %apply_first.1.refs_7_ = f32[256,256]{1,0:T(8,128)} custom-call(s32[1]{0:T(128)} %bitcast.9.h.head_ref, s32[4]{0:T(128)} %pad_add_fusion.order_ref, f32[4,64,512]{2,1,0:T(8,128)} %pad_maximum_fusion.1.qa.qb.qc.qd.refs_0_.refs_1_.refs_2_.refs_3_, f32[4,64,512]{2,1,0:T(8,128)} %pad_maximum_fusion.1.qa.qb.qc.qd.refs_0_.refs_1_.refs_2_.refs_3_, ...), custom_call_target="tpu_custom_call" | custom-call | tf_op jit(solution)/shard_map/apply_first/pallas_call | solution.py:204
  178.2 4.3 %apply_second.1 = bf16[256,512]{1,0:T(8,128)(2,1)} custom-call(s32[1]{0:T(128)} %bitcast.h.head_ref, s32[4]{0:T(128)} %pad_add_fusion.order_ref, f32[4,64,512]{2,1,0:T(8,128)} %pad_maximum_fusion.1.qa.qb.qc.qd.refs_0_.refs_1_.refs_2_.refs_3_, f32[4,64,512]{2,1,0:T(8,128)} %pad_maximum_fusion.1.qa.qb.qc.qd.refs_0_.refs_1_.refs_2_.refs_3_, ...), custom_call_target="tpu_custom_call" | custom-call | tf_op jit(solution)/shard_map/apply_second/pallas_call | solution.py:204
  182.5 5.5 %fusion = f32[256,4096]{1,0:T(8,128)} fusion(bf16[256,512]{1,0:T(8,128)(2,1)} %apply_second.1, bf16[512,4096]{1,0:T(8,128)(2,1)} %param.13), kind=kOutput, calls=%fused_computation.10 | convolution fusion | flops 1073741824 | bytes 8650752 | tf_op jit(solution)/shard_map/dot_general | solution.py:276
  189.4 2.5 maximum_select_fusion
  191.9 2.2 copy.14
  194.1 71.9 %reduce-scatter.2.cloned.1.call-done = f32[64,4096]{1,0:T(8,128)} async-done(((f32[256,4096]{1,0:T(8,128)}), f32[64,4096]{1,0:T(8,128)}) %reduce-scatter.2.cloned.1.call-update) | async-done | bytes 1048592 | tf_op jit(solution)/shard_map/reduce_scatter | solution.py:277
  266.0 2.1 convert_element_type.3
  (29 shorter events, 9.2 us)
Async XLA Ops:
  7.2 8.8 %copy-start.5 = (f32[2,256]{1,0:T(2,128)S(1)}, f32[2,256]{1,0:T(2,128)}, u32[]{:S(2)}) copy-start(f32[2,256]{1,0:T(2,128)} %param.10) | copy-start | bytes 6148
  9.5 31.7 %all-to-all-start = ((f32[4,2,64,512]{3,2,1,0:T(8,128)}), f32[4,2,64,512]{3,2,1,0:T(8,128)S(1)}, u32[]{:S(2)}, u32[]{:S(2)}) async-start(f32[4,2,64,512]{3,2,1,0:T(8,128)} %pad_maximum_fusion), calls=%async_computation | async-start | bytes 2097152 | tf_op jit(solution)/shard_map/all_to_all | solution.py:225
  15.9 250.1 %reduce-scatter.2.cloned.1.call-start = ((), (), s32[]{:S(2)}) async-start(), calls=%async_computation.4 | async-start | bytes 5242880 | tf_op jit(solution)/shard_map/reduce_scatter | solution.py:277
  41.2 1.0 copy-start
  46.5 5.7 %collective-permute-start.3 = (f32[3,256,512]{2,1,0:T(8,128)}, f32[3,256,512]{2,1,0:T(8,128)S(1)}, u32[]{:S(2)}, u32[]{:S(2)}) collective-permute-start(f32[3,256,512]{2,1,0:T(8,128)} %gradient.3), channel_id=1, source_target_pairs={{0,4},{4,0},{1,5},{5,1},{2,6},{6,2},{3,7},{7,3},{8,12},{12,8},{9,1... | collective-permute-start | bytes 4718600 | tf_op jit(solution)/shard_map/ppermute | solution.py:243
  82.1 7.6 %collective-permute-start.4 = (f32[48,512]{1,0:T(8,128)S(1)}, f32[48,512]{1,0:T(8,128)S(1)}, u32[]{:S(2)}, u32[]{:S(2)}) collective-permute-start(f32[48,512]{1,0:T(8,128)S(1)} %reduce_sum.9), channel_id=1, source_target_pairs={{0,8},{8,0},{1,9},{9,1},{2,10},{10,2},{3,11},{11,3},{4,12},{12,4},... | collective-permute-start | bytes 294920 | tf_op jit(solution)/shard_map/ppermute | solution.py:250
  111.7 14.9 %copy-start.1 = (f32[4,2,64,512]{3,2,1,0:T(8,128)S(1)}, f32[4,2,64,512]{3,2,1,0:T(8,128)}, u32[]{:S(2)}) copy-start(f32[4,2,64,512]{3,2,1,0:T(8,128)} %copy-done) | copy-start | bytes 3145732
  111.7 21.5 %copy-start.4 = (f32[64,2048]{1,0:T(8,128)S(1)}, f32[64,2048]{1,0:T(8,128)}, u32[]{:S(2)}) copy-start(f32[64,2048]{1,0:T(8,128)} %param.7) | copy-start | bytes 1572868
  120.6 56.4 %collective-permute-start.5 = (f32[3,256,512]{2,1,0:T(8,128)}, f32[3,256,512]{2,1,0:T(8,128)S(1)}, u32[]{:S(2)}, u32[]{:S(2)}) collective-permute-start(f32[3,256,512]{2,1,0:T(8,128)} %newton.1.refs_4_), channel_id=1, source_target_pairs={{0,4},{4,0},{1,5},{5,1},{2,6},{6,2},{3,7},{7,3},{8,12},{12,8},{9,1... | collective-permute-start | bytes 4718600 | tf_op jit(solution)/shard_map/ppermute | solution.py:243
  126.6 41.0 %collective-permute-start.6 = (f32[4,2,64,512]{3,2,1,0:T(8,128)S(1)}, f32[4,2,64,512]{3,2,1,0:T(8,128)}, u32[]{:S(2)}, u32[]{:S(2)}) collective-permute-start(f32[4,2,64,512]{3,2,1,0:T(8,128)S(1)} %copy-done.1), channel_id=1, source_target_pairs={{0,4},{4,8},{8,12},{12,16},{16,20},{20,24},{24,28},{28,32},{32,36}... | collective-permute-start | bytes 3145736 | tf_op jit(solution)/shard_map/ppermute | solution.py:255
  133.9 27.0 %collective-permute-start = (f32[64,512]{1,0:T(8,128)}, f32[64,512]{1,0:T(8,128)S(1)}, u32[]{:S(2)}, u32[]{:S(2)}) collective-permute-start(f32[64,512]{1,0:T(8,128)} %get-tuple-element.7), channel_id=1, source_target_pairs={{0,1},{1,2},{2,3},{3,0},{4,5},{5,6},{6,7},{7,4},{8,9},{9,10},{10,1... | collective-permute-start | bytes 393224 | tf_op jit(solution)/shard_map/ppermute | solution.py:236
  134.0 27.0 %collective-permute-start.2 = (f32[64,512]{1,0:T(8,128)S(1)}, f32[64,512]{1,0:T(8,128)S(1)}, u32[]{:S(2)}, u32[]{:S(2)}) collective-permute-start(f32[64,512]{1,0:T(8,128)S(1)} %get-tuple-element.8), channel_id=1, source_target_pairs={{0,3},{1,0},{2,1},{3,2},{4,7},{5,4},{6,5},{7,6},{8,11},{9,8},{10,9... | collective-permute-start | bytes 393224 | tf_op jit(solution)/shard_map/ppermute | solution.py:236
  137.2 29.5 %collective-permute-start.1 = (f32[64,512]{1,0:T(8,128)S(1)}, f32[64,512]{1,0:T(8,128)S(1)}, u32[]{:S(2)}, u32[]{:S(2)}) collective-permute-start(f32[64,512]{1,0:T(8,128)S(1)} %get-tuple-element.9), channel_id=1, source_target_pairs={{0,2},{1,3},{2,0},{3,1},{4,6},{5,7},{6,4},{7,5},{8,10},{9,11},{10,... | collective-permute-start | bytes 393224 | tf_op jit(solution)/shard_map/ppermute | solution.py:236
  177.0 1.2 copy-start.3
  188.0 1.4 copy-start.2
Sparse Core Ops, SparseCore 0:
  188.2 77.8 reduce-scatter.1
